TPU v7x, 32 devices: a whole 2x2x4 slice. The times are simulated.
32 devices in a mesh: depth: 8 (over z, core), freq: 4 (over y, x).
Axes of the slice: x: 2, y: 2, z: 4, core: 2. Of those that a mesh axis runs over, the one named last changes fastest.
Arguments:
- fields_top: bfloat16 [8, 2, 4, 2, 384, 384], P('depth', None, 'freq'), may hold values from -6 to 6
- surface: bfloat16 [2, 2, 4, 2, 384, 384], P(None, None, 'freq'), may hold values from -6 to 6
- up_state: bfloat16 [8, 4, 2, 384, 384], P('depth', 'freq'), may hold values from -6 to 6
- angular_freq: float32 [4], P('freq'), may hold values from 0.5 to 2.5
- class_slowness: float32 [8], replicated, may hold values from 0.6 to 1.3
- velocity_class: int32 [8, 12, 12], P('depth'), may hold values from 0 to 7
- slowness_detail: float32 [8, 384, 384], P('depth'), may hold values from 0.5 to 1.5
Outputs:
- reflectivity: bfloat16 [8, 384, 384], P('depth', 'freq')
- up_out: bfloat16 [8, 4, 2, 384, 384], P('depth', 'freq')
All inputs are finite; a program needn't handle non-finite values.
Results may differ from a plain program's by a relative error of at most 0.023.
Values may be sent and summed in bfloat16 or wider, within the bound.
A program may use at most 64 MiB of HBM per device.

v0:
```python
import jax
import jax.numpy as jnp
from jax import lax
from jax.sharding import PartitionSpec as P

LAYERS = 1
TICKS = 3
CLASSES = 8
BLOCK = 32
DEPTH_STEP = 1.0
EPSILON = 1e-06


def passed_along(block, axis, distance):
    devices = range(lax.axis_size(axis))
    route = [(i - distance, i) for i in devices if i - distance in devices]
    return lax.ppermute(block, axis, route)


def make_tables(lateral):
    positions = jnp.arange(lateral, dtype=jnp.int32)
    wrapped = positions[:, None] * positions[None, :] % lateral
    angles = wrapped.astype(jnp.float32) * (2.0 * jnp.pi / lateral)
    cosine_table = jnp.cos(angles).astype(jnp.bfloat16)
    sine_table = jnp.sin(angles).astype(jnp.bfloat16)
    folded = jnp.where(positions < lateral // 2, positions, positions - lateral)
    kappa = folded.astype(jnp.float32) * (2.0 * jnp.pi / lateral)
    wavenumber_sq = kappa[:, None] ** 2 + kappa[None, :] ** 2
    return (cosine_table, sine_table, wavenumber_sq)


def cell_slowness(velocity_class, class_slowness, slowness_detail):
    count, lateral = (slowness_detail.shape[0], slowness_detail.shape[1])
    blocks = lateral // BLOCK
    onehot = (velocity_class[..., None] == jnp.arange(CLASSES, dtype=jnp.int32)).astype(jnp.float32)
    block_slow = jnp.sum(onehot * class_slowness, axis=-1)
    spread = jnp.broadcast_to(
        block_slow[:, :, None, :, None], (count, blocks, BLOCK, blocks, BLOCK)
    )
    slowness = spread.reshape(count, lateral, lateral) * slowness_detail
    return (slowness, jnp.mean(slowness, axis=(1, 2)))


def propagate(
    real_part, imag_part, angular, slowness, reference_slow, cosine_table, sine_table, wavenumber_sq
):
    lateral = real_part.shape[0]
    joined_cols = jnp.concatenate([cosine_table, sine_table], axis=1)
    joined_rows = jnp.concatenate([cosine_table, sine_table], axis=0)
    product = jnp.dot(
        jnp.concatenate([real_part, imag_part], axis=0),
        joined_cols,
        preferred_element_type=jnp.float32,
    )
    real_cos, real_sin = (product[:lateral, :lateral], product[:lateral, lateral:])
    imag_cos, imag_sin = (product[lateral:, :lateral], product[lateral:, lateral:])
    half_real = (real_cos + imag_sin).astype(jnp.bfloat16)
    half_imag = (imag_cos - real_sin).astype(jnp.bfloat16)
    product = jnp.dot(
        joined_rows,
        jnp.concatenate([half_real, half_imag], axis=1),
        preferred_element_type=jnp.float32,
    )
    cos_real, cos_imag = (product[:lateral, :lateral], product[:lateral, lateral:])
    sin_real, sin_imag = (product[lateral:, :lateral], product[lateral:, lateral:])
    spec_real = cos_real + sin_imag
    spec_imag = cos_imag - sin_real
    vertical = (angular * reference_slow) ** 2 - wavenumber_sq
    travel = jnp.sqrt(jnp.maximum(vertical, 0.0)) * DEPTH_STEP
    decay = jnp.exp(-jnp.sqrt(jnp.maximum(-vertical, 0.0)) * DEPTH_STEP) / (lateral * lateral)
    phase_real = decay * jnp.cos(travel)
    phase_imag = decay * jnp.sin(travel)
    shifted_real = (spec_real * phase_real - spec_imag * phase_imag).astype(jnp.bfloat16)
    shifted_imag = (spec_real * phase_imag + spec_imag * phase_real).astype(jnp.bfloat16)
    product = jnp.dot(
        joined_rows,
        jnp.concatenate([shifted_real, shifted_imag], axis=1),
        preferred_element_type=jnp.float32,
    )
    cos_real, cos_imag = (product[:lateral, :lateral], product[:lateral, lateral:])
    sin_real, sin_imag = (product[lateral:, :lateral], product[lateral:, lateral:])
    back_real = (cos_real - sin_imag).astype(jnp.bfloat16)
    back_imag = (cos_imag + sin_real).astype(jnp.bfloat16)
    product = jnp.dot(
        jnp.concatenate([back_real, back_imag], axis=0),
        joined_cols,
        preferred_element_type=jnp.float32,
    )
    real_cos, real_sin = (product[:lateral, :lateral], product[:lateral, lateral:])
    imag_cos, imag_sin = (product[lateral:, :lateral], product[lateral:, lateral:])
    space_real = real_cos - imag_sin
    space_imag = imag_cos + real_sin
    lens = angular * DEPTH_STEP * (slowness - reference_slow)
    lens_cos, lens_sin = (jnp.cos(lens), jnp.sin(lens))
    new_real = (space_real * lens_cos - space_imag * lens_sin).astype(jnp.bfloat16)
    new_imag = (space_real * lens_sin + space_imag * lens_cos).astype(jnp.bfloat16)
    return (new_real, new_imag)


def advance(fields, angular, slowness, reference_slow, tables):
    cosine_table, sine_table, wavenumber_sq = tables

    def single(real_part, imag_part, frequency):
        return propagate(
            real_part,
            imag_part,
            frequency,
            slowness,
            reference_slow,
            cosine_table,
            sine_table,
            wavenumber_sq,
        )

    new_real, new_imag = jax.vmap(single)(fields[:, 0], fields[:, 1], angular)
    return jnp.stack([new_real, new_imag], axis=1)


def advance_pair(fields, angular, slowness, reference_slow, tables):

    def one_field(member):
        return advance(member, angular, slowness, reference_slow, tables)

    return jax.vmap(one_field)(fields)


def image_terms(fields):
    source = fields[0].astype(jnp.float32)
    receiver = fields[1].astype(jnp.float32)
    image_part = jnp.sum(source[:, 0] * receiver[:, 0] + source[:, 1] * receiver[:, 1], axis=0)
    illum_part = jnp.sum(source[:, 0] * source[:, 0] + source[:, 1] * source[:, 1], axis=0)
    return (image_part, illum_part)


def per_device(
    fields_top, surface, up_state, angular_freq, class_slowness, velocity_class, slowness_detail
):
    lateral = fields_top.shape[-1]
    tables = make_tables(lateral)
    slowness, reference_slow = cell_slowness(velocity_class, class_slowness, slowness_detail)
    segment_index = lax.axis_index("depth")
    image_sum = [jnp.zeros((lateral, lateral), jnp.float32)]
    illumination = [jnp.zeros((lateral, lateral), jnp.float32)]
    sources = [None] * LAYERS
    fields = fields_top[0]
    for turn_index in range(TICKS):
        layer_index = 0
        fields = advance_pair(
            fields, angular_freq, slowness[layer_index], reference_slow[layer_index], tables
        )
        image_part, illum_part = image_terms(fields)
        image_sum[layer_index] = image_sum[layer_index] + image_part
        illumination[layer_index] = illumination[layer_index] + illum_part
        if turn_index == TICKS - 1:
            sources[layer_index] = fields[0]
        if turn_index + 1 < TICKS:
            from_above = passed_along(fields, "depth", 1)
            fields = jnp.where(segment_index == 0, surface[turn_index], from_above)
    image_all = jnp.stack(image_sum)
    illum_all = jnp.stack(illumination)
    image_total, illum_total = (
        lax.psum(image_all.astype(jnp.bfloat16), "freq").astype(jnp.float32),
        lax.psum(illum_all.astype(jnp.bfloat16), "freq").astype(jnp.float32),
    )
    damping = jnp.mean(illum_total, axis=(1, 2))
    balanced = image_total / (illum_total + damping[:, None, None])
    mean_square = jnp.mean(balanced * balanced, axis=(1, 2))
    reflect = (balanced * lax.rsqrt(mean_square + EPSILON)[:, None, None]).astype(jnp.bfloat16)
    row_count = lateral // lax.axis_size("freq")
    reflect_part = lax.dynamic_slice_in_dim(
        reflect, lax.axis_index("freq") * row_count, row_count, 1
    )
    rising_wave = passed_along(up_state[0], "depth", -1)
    for layer_index in reversed(range(LAYERS)):
        scattered = reflect[layer_index].astype(jnp.float32)[None, None] * sources[
            layer_index
        ].astype(jnp.float32)
        rising_wave = (rising_wave.astype(jnp.float32) + scattered).astype(jnp.bfloat16)
        rising_wave = advance(
            rising_wave, angular_freq, slowness[layer_index], reference_slow[layer_index], tables
        )
    return (reflect_part, rising_wave[None])


def solution(mesh):
    return jax.shard_map(
        per_device,
        mesh=mesh,
        in_specs=(
            P("depth", None, "freq", None, None, None),
            P(None, None, "freq", None, None, None),
            P("depth", "freq", None, None, None),
            P("freq"),
            P(),
            P("depth", None, None),
            P("depth", None, None),
        ),
        out_specs=(P("depth", "freq", None), P("depth", "freq", None, None, None)),
        check_vma=False,
    )
```

profile of v0, /device:TPU:0, one launch (start us, length us, event | category | flops | bytes accessed | tf_op | source)
XLA Modules:
  0.0 157.0 jit_solution(17389596648066102286)
XLA Ops:
  7.2 2.6 %sine_convert_fusion = (bf16[384,384]{0,1:T(8,128)(2,1)S(1)}, bf16[384,384]{0,1:T(8,128)(2,1)S(1)}) fusion(), kind=kLoop, calls=%fused_computation.237 | loop fusion | flops 1622016 | bytes 589824 | tf_op jit(solution)/shard_map/convert_element_type | solution.py:25
  9.8 0.7 copy.102
  10.5 0.7 select_reduce_fusion
  11.2 1.9 %broadcast_in_dim.6 = f32[12,32,12,32]{3,2,1,0:T(8,128)} broadcast(f32[12,12]{1,0:T(8,128)S(1)} %select_reduce_fusion), dimensions={0,2} | broadcast | bytes 590400 | tf_op jit(solution)/shard_map/broadcast_in_dim | solution.py:37
  13.1 2.5 %broadcast_in_dim.7 = f32[1,384,384]{2,1,0:T(8,128)S(1)} reshape(f32[12,32,12,32]{3,2,1,0:T(8,128)} %broadcast_in_dim.6) | data formatting | bytes 1179648 | tf_op jit(solution)/shard_map/broadcast_in_dim | solution.py:37
  16.4 0.8 fusion.140
  18.1 1.4 convolution_bitcast_fusion.11
  19.5 0.3 fusion.11
  19.8 2.6 %cosine_multiply_fusion.1 = (f32[384,384]{0,1:T(8,128)S(1)}, f32[384,384]{0,1:T(8,128)S(1)}) fusion(f32[384]{0:T(512)S(1)} %fusion.123, f32[]{:T(128)} %bitcast.11), kind=kLoop, calls=%fused_computation.233 | loop fusion | flops 1327104 | bytes 1181188 | tf_op jit(solution)/shard_map/vmap(vmap())/mul | solution.py:71
  22.3 1.4 convolution_bitcast_fusion.10
  23.7 0.4 fusion.41
  24.1 1.4 convolution_bitcast_fusion.9
  25.8 2.3 %fusion.113 = (f32[384,384]{1,0:T(8,128)S(1)}, f32[384,384]{1,0:T(8,128)S(1)}) fusion(f32[1,384,384]{2,1,0:T(8,128)S(1)} %get-tuple-element.7, f32[]{:T(128)} %div.22, f32[]{:T(128)} %bitcast.257), kind=kLoop, calls=%fused_computation.245 | loop fusion | flops 294912 | bytes 1769480 | tf_op jit(solution)/shard_map/vmap(vmap())/mul | solution.py:95
  28.1 1.4 convolution_bitcast_fusion.8
  29.6 0.4 fusion.43
  30.0 1.2 pad_maximum_fusion
  31.2 3.4 %collective-permute-start = (bf16[2,1,2,384,384]{4,3,0,2,1:T(8,128)(2,1)}, bf16[2,1,2,384,384]{4,3,0,2,1:T(8,128)(2,1)}, u32[]{:S(2)}, u32[]{:S(2)}) collective-permute-start(bf16[2,1,2,384,384]{4,3,0,2,1:T(8,128)(2,1)} %pad_maximum_fusion), channel_id=1, source_target_pairs={{0,4},{4,8},{8,12},{12,16},{16,20},{20,24},{24,28},{1,5},{5,9},{9,... | collective-permute-start | bytes 3538952 | tf_op jit(solution)/shard_map/ppermute | solution.py:17
  34.6 1.9 %fusion.141 = (bf16[1,2,1,2,384,384]{5,4,3,2,1,0:T(8,128)(2,1)S(1)}, bf16[1,2,1,2,384,384]{5,4,3,2,1,0:T(8,128)(2,1)S(1)}) fusion(bf16[2,2,1,2,384,384]{5,4,3,2,1,0:T(8,128)(2,1)} %param.8), kind=kLoop, calls=%fused_computation.281 | loop fusion | bytes 4718592 | tf_op jit(solution)/shard_map/slice | solution.py:158
  36.8 1.4 convolution_bitcast_fusion.7
  38.2 0.3 fusion.7
  38.5 1.4 convolution_bitcast_fusion.6
  39.9 0.4 fusion.45
  40.3 1.4 convolution_bitcast_fusion.5
  42.0 1.4 convolution_bitcast_fusion.4
  43.4 0.4 fusion.47
  44.0 16.8 %collective-permute-start.1 = (bf16[2,1,2,384,384]{4,3,0,2,1:T(8,128)(2,1)S(1)}, bf16[2,1,2,384,384]{4,3,0,2,1:T(8,128)(2,1)S(1)}, u32[]{:S(2)}, u32[]{:S(2)}) collective-permute-start(bf16[2,1,2,384,384]{4,3,0,2,1:T(8,128)(2,1)S(1)} %pad_maximum_fusion.1), channel_id=1, source_target_pairs={{0,4},{4,8},{8,12},{12,16},{16,20},{20,24},{24,28},{1,5},{5,9},{9,... | collective-permute-start | bytes 3538952 | tf_op jit(solution)/shard_map/ppermute | solution.py:17
  61.1 1.8 %collective-permute-done.1 = bf16[2,1,2,384,384]{4,3,0,2,1:T(8,128)(2,1)S(1)} collective-permute-done((bf16[2,1,2,384,384]{4,3,0,2,1:T(8,128)(2,1)S(1)}, bf16[2,1,2,384,384]{4,3,0,2,1:T(8,128)(2,1)S(1)}, u32[]{:S(2)}, u32[]{:S(2)}) %collective-permute-start.1) | collective-permute-done | bytes 1179680 | tf_op jit(solution)/shard_map/ppermute | solution.py:17
  63.2 1.4 convolution_bitcast_fusion.3
  64.9 1.4 convolution_bitcast_fusion.2
  66.3 0.4 fusion.49
  66.7 1.4 convolution_bitcast_fusion.1
  68.4 1.4 convolution_bitcast_fusion
  69.8 0.4 fusion.52
  70.4 1.3 fusion.120
  71.7 1.6 collective-permute-start.2
  73.3 59.8 %all-reduce.3.cloned.1.call-done = (bf16[1,384,384]{2,1,0:T(8,128)(2,1)}, bf16[1,384,384]{2,1,0:T(8,128)(2,1)}) async-done(((bf16[1,384,384]{2,1,0:T(8,128)(2,1)}, bf16[1,384,384]{2,1,0:T(8,128)(2,1)}), (bf16[1,384,384]{2,1,0:T(8,128)(2,1)}, bf16[1,384,384]{2,1,0:T(8,128)(2,1)})) %all-reduce.3.cloned.1.call-update) | async-done | bytes 589840 | tf_op jit(solution)/shard_map/psum | solution.py:163
  133.1 1.7 %convert_reduce_fusion = f32[]{:T(128)} fusion(bf16[1,384,384]{2,1,0:T(8,128)(2,1)} %get-tuple-element.2), kind=kLoop, calls=%fused_computation.120 | loop fusion | flops 294911 | bytes 294916 | tf_op jit(solution)/shard_map/reduce_sum | solution.py:165
  135.5 1.8 %multiply_reduce_fusion = f32[]{:T(128)} fusion(f32[]{:T(128)S(6)} %div.25, bf16[1,384,384]{2,1,0:T(8,128)(2,1)} %get-tuple-element.2, bf16[1,384,384]{2,1,0:T(8,128)(2,1)} %get-tuple-element.3), kind=kLoop, calls=%fused_computation.229 | loop fusion | flops 884735 | bytes 589832 | tf_op jit(solution)/shard_map/reduce_sum | solution.py:167
  138.0 1.2 bitcast_convert_fusion
  139.5 0.8 convolution_bitcast_fusion.15
  140.4 0.8 convolution_bitcast_fusion.12
  141.1 3.1 %subtract_convert_fusion.7 = (bf16[1,384,384]{1,2,0:T(8,128)(2,1)S(1)}, bf16[1,384,384]{1,2,0:T(8,128)(2,1)S(1)}) fusion(f32[384]{0:T(512)S(1)} %fusion.123, f32[]{:T(128)} %bitcast.11, f32[768,1,768]{0,2,1:T(8,128)S(1)} %convolution_bitcast_fusion.12), kind=kLoop, calls=%fused_computation.222 | loop fusion | flops 2801664 | bytes 2953220 | tf_op jit(solution)/shard_map/vmap()/convert_element_type | solution.py:73
  144.3 0.8 convolution_bitcast_fusion.14
  145.2 0.6 constant_dynamic-slice_fusion
  145.9 0.8 convolution_bitcast_fusion.13
  146.7 0.3 copy-done.3
  146.9 2.3 %fusion.117 = (bf16[1,1,384,384]{3,2,1,0:T(8,128)(2,1)S(1)}, bf16[1,1,384,384]{3,2,1,0:T(8,128)(2,1)S(1)}) fusion(f32[1,384,384]{2,1,0:T(8,128)S(1)} %copy-done.3, f32[]{:T(128)} %div.22, f32[]{:T(128)} %bitcast.258, f32[1,768,768]{2,1,0:T(8,128)S(1)} %convolution_bitcast_fusion.13), kind=kLoop, calls=%fused_computation.252 | loop fusion | flops 1769472 | bytes 3538952 | tf_op jit(solution)/shard_map/stack | solution.py:116
  149.3 0.9 maximum_bitcast_fusion.32
  (36 shorter events, 3.0 us)
Async XLA Ops:
  7.2 125.9 %all-reduce.3.cloned.1.call-start = ((), (), s32[]{:S(2)}) async-start(), calls=%async_computation | async-start | bytes 1179648 | tf_op jit(solution)/shard_map/psum | solution.py:163
  13.1 3.3 %copy-start.5 = (f32[1,384,384]{2,1,0:T(8,128)S(1)}, f32[1,384,384]{2,1,0:T(8,128)}, u32[]{:S(2)}) copy-start(f32[1,384,384]{2,1,0:T(8,128)} %param.13) | copy-start | bytes 1769476
  15.6 2.2 %copy-start.4 = (bf16[1,2,1,2,384,384]{5,4,3,2,1,0:T(8,128)(2,1)S(1)}, bf16[1,2,1,2,384,384]{5,4,3,2,1,0:T(8,128)(2,1)}, u32[]{:S(2)}) copy-start(bf16[1,2,1,2,384,384]{5,4,3,2,1,0:T(8,128)(2,1)} %param.7) | copy-start | bytes 3538948
  17.1 8.7 %copy-start.2 = (f32[1,384,384]{2,1,0:T(8,128)}, f32[1,384,384]{2,1,0:T(8,128)S(1)}, u32[]{:S(2)}) copy-start(f32[1,384,384]{2,1,0:T(8,128)S(1)} %get-tuple-element.7) | copy-start | bytes 1769476
  30.0 1.2 copy-start
  31.2 5.3 %collective-permute-start = (bf16[2,1,2,384,384]{4,3,0,2,1:T(8,128)(2,1)}, bf16[2,1,2,384,384]{4,3,0,2,1:T(8,128)(2,1)}, u32[]{:S(2)}, u32[]{:S(2)}) collective-permute-start(bf16[2,1,2,384,384]{4,3,0,2,1:T(8,128)(2,1)} %pad_maximum_fusion), channel_id=1, source_target_pairs={{0,4},{4,8},{8,12},{12,16},{16,20},{20,24},{24,28},{1,5},{5,9},{9,... | collective-permute-start | bytes 3538952 | tf_op jit(solution)/shard_map/ppermute | solution.py:17
  43.8 17.0 %copy-start.1 = (bf16[2,1,1,384,384]{4,3,0,2,1:T(8,128)(2,1)S(1)}, bf16[2,1,1,384,384]{4,3,0,2,1:T(8,128)(2,1)}, u32[]{:S(2)}) copy-start(bf16[2,1,1,384,384]{4,3,0,2,1:T(8,128)(2,1)} %copy-done) | copy-start | bytes 1769476
  44.0 19.0 %collective-permute-start.1 = (bf16[2,1,2,384,384]{4,3,0,2,1:T(8,128)(2,1)S(1)}, bf16[2,1,2,384,384]{4,3,0,2,1:T(8,128)(2,1)S(1)}, u32[]{:S(2)}, u32[]{:S(2)}) collective-permute-start(bf16[2,1,2,384,384]{4,3,0,2,1:T(8,128)(2,1)S(1)} %pad_maximum_fusion.1), channel_id=1, source_target_pairs={{0,4},{4,8},{8,12},{12,16},{16,20},{20,24},{24,28},{1,5},{5,9},{9,... | collective-permute-start | bytes 3538952 | tf_op jit(solution)/shard_map/ppermute | solution.py:17
  70.4 1.3 copy-start.6
  71.7 67.5 %collective-permute-start.2 = (bf16[1,2,384,384]{3,2,1,0:T(8,128)(2,1)S(1)}, bf16[1,2,384,384]{3,2,1,0:T(8,128)(2,1)S(1)}, u32[]{:S(2)}, u32[]{:S(2)}) collective-permute-start(bf16[1,2,384,384]{3,2,1,0:T(8,128)(2,1)S(1)} %bitcast.261), channel_id=1, source_target_pairs={{4,0},{8,4},{12,8},{16,12},{20,16},{24,20},{28,24},{5,1},{9,5},{13... | collective-permute-start | bytes 1769480 | tf_op jit(solution)/shard_map/ppermute | solution.py:17
  145.9 1.1 copy-start.3
Sparse Core Ops, SparseCore 0:
  71.8 61.2 all-reduce.2
where the time goes:
time: 157 us
  waiting for transfers between devices  61.7 us (39%)
  other arithmetic  27.7 us (18%)
  starting transfers between devices  21.8 us (14%)
  matrix products  20.2 us (13%)
  between operations  17.2 us (11%)
  local copies, waits for them, and re-layouts  8.43 us (5%)
    psum x1, waiting for transfers between devices, per_device(): lax.psum(illum_all.astype(jnp.bfloat16), 'freq').astype(jnp.float32)  59.8 us
    ppermute x3, starting transfers between devices, passed_along(): return lax.ppermute(block, axis, route)  21.8 us
    dot_general x4, matrix products, propagate(): jnp.dot(joined_rows, jnp.concatenate([shifted_real, shifted_imag], axis=1...  5.13 us
    dot_general x4, matrix products, propagate(): jnp.dot(jnp.concatenate([back_real, back_imag], axis=0), joined_cols, pre...  5.05 us
    dot_general x4, matrix products, propagate(): jnp.dot(jnp.concatenate([real_part, imag_part], axis=0), joined_cols, pre...  5.05 us
    dot_general x4, matrix products, propagate(): jnp.dot(joined_rows, jnp.concatenate([half_real, half_imag], axis=1), pre...  4.96 us
    another operation x6, other arithmetic, advance(): return jnp.stack([new_real, new_imag], axis=1)  4.86 us
    broadcast_in_dim x2, local copies, waits for them, and re-layouts, cell_slowness(): jnp.broadcast_to(block_slow[:, :, None, :, None], (count, blocks, BLOCK,...  4.38 us
  transfers between devices with their start and end apart: 4, of which 2 were waited for; matrix products, arithmetic and copies ran while one was open for 4% of the time, Pallas kernels for 0%

commit v1 on v0

--- a/solution.py
+++ b/solution.py
@@ -158,9 +158,13 @@
             fields = jnp.where(segment_index == 0, surface[turn_index], from_above)
     image_all = jnp.stack(image_sum)
     illum_all = jnp.stack(illumination)
+
+    def proceed_fields_in(vec):
+        return lax.all_gather(vec, "freq").sum(axis=0)
+
     image_total, illum_total = (
         lax.psum(image_all.astype(jnp.bfloat16), "freq").astype(jnp.float32),
-        lax.psum(illum_all.astype(jnp.bfloat16), "freq").astype(jnp.float32),
+        proceed_fields_in(illum_all.astype(jnp.bfloat16)).astype(jnp.float32),
     )
     damping = jnp.mean(illum_total, axis=(1, 2))
     balanced = image_total / (illum_total + damping[:, None, None])

time: 157 us -> 183 us (1.17)
  waiting for transfers between devices: 61.7 us -> 87 us
    all_gather x0 -> x1, waiting for transfers between devices: none -> 40.6 us  [proceed_fields_in(): return lax.all_gather(vec, 'freq').sum(axis=0)]
    psum x1, waiting for transfers between devices: 59.8 us -> 43.9 us  [per_device(): lax.psum(image_all.astype(jnp.bfloat16), 'freq').astype(jnp.float32)]
  transfers between devices with their start and end apart: 4 -> 5, of which waited for: 2 -> 3; matrix products, arithmetic and copies ran while one was open for 4% -> 4% of each run, Pallas kernels for 0% -> 0%
where the time goes in v1:
time: 183 us
  waiting for transfers between devices  87 us (48%)
  other arithmetic  28.2 us (15%)
  starting transfers between devices  21.9 us (12%)
  matrix products  20.2 us (11%)
  between operations  17.2 us (9%)
  local copies, waits for them, and re-layouts  8.44 us (5%)
    psum x1, waiting for transfers between devices, per_device(): lax.psum(image_all.astype(jnp.bfloat16), 'freq').astype(jnp.float32)  43.9 us
    all_gather x1, waiting for transfers between devices, proceed_fields_in(): return lax.all_gather(vec, 'freq').sum(axis=0)  40.6 us
    ppermute x3, starting transfers between devices, passed_along(): return lax.ppermute(block, axis, route)  21.8 us
    dot_general x4, matrix products, propagate(): jnp.dot(joined_rows, jnp.concatenate([shifted_real, shifted_imag], axis=1...  5.12 us
    dot_general x4, matrix products, propagate(): jnp.dot(jnp.concatenate([back_real, back_imag], axis=0), joined_cols, pre...  5.05 us
    dot_general x4, matrix products, propagate(): jnp.dot(jnp.concatenate([real_part, imag_part], axis=0), joined_cols, pre...  5.04 us
    dot_general x4, matrix products, propagate(): jnp.dot(joined_rows, jnp.concatenate([half_real, half_imag], axis=1), pre...  4.96 us
    another operation x6, other arithmetic, advance(): return jnp.stack([new_real, new_imag], axis=1)  4.89 us
  transfers between devices with their start and end apart: 5, of which 3 were waited for; matrix products, arithmetic and copies ran while one was open for 4% of the time, Pallas kernels for 0%

profile of v1, /device:TPU:0, one launch (start us, length us, event | category | flops | bytes accessed | tf_op | source)
XLA Modules:
  0.0 182.9 jit_solution(16351738295677186470)
XLA Ops:
  7.2 2.6 %sine_convert_fusion = (bf16[384,384]{0,1:T(8,128)(2,1)S(1)}, bf16[384,384]{0,1:T(8,128)(2,1)S(1)}) fusion(), kind=kLoop, calls=%fused_computation.238 | loop fusion | flops 1622016 | bytes 589824 | tf_op jit(solution)/shard_map/convert_element_type | solution.py:25
  9.8 0.7 copy.121
  10.5 0.7 select_reduce_fusion
  11.2 1.9 %broadcast_in_dim.6 = f32[12,32,12,32]{3,2,1,0:T(8,128)} broadcast(f32[12,12]{1,0:T(8,128)S(1)} %select_reduce_fusion), dimensions={0,2} | broadcast | bytes 590400 | tf_op jit(solution)/shard_map/broadcast_in_dim | solution.py:37
  13.1 2.5 %broadcast_in_dim.7 = f32[1,384,384]{2,1,0:T(8,128)S(1)} reshape(f32[12,32,12,32]{3,2,1,0:T(8,128)} %broadcast_in_dim.6) | data formatting | bytes 1179648 | tf_op jit(solution)/shard_map/broadcast_in_dim | solution.py:37
  16.4 0.8 fusion.140
  18.1 1.4 convolution_bitcast_fusion.11
  19.8 2.6 %cosine_multiply_fusion.1 = (f32[384,384]{0,1:T(8,128)S(1)}, f32[384,384]{0,1:T(8,128)S(1)}) fusion(f32[384]{0:T(512)S(1)} %fusion.123, f32[]{:T(128)} %bitcast.11), kind=kLoop, calls=%fused_computation.234 | loop fusion | flops 1327104 | bytes 1181188 | tf_op jit(solution)/shard_map/vmap(vmap())/mul | solution.py:71
  22.3 1.4 convolution_bitcast_fusion.10
  23.7 0.4 fusion.42
  24.1 1.4 convolution_bitcast_fusion.9
  25.8 2.3 %fusion.114 = (f32[384,384]{1,0:T(8,128)S(1)}, f32[384,384]{1,0:T(8,128)S(1)}) fusion(f32[1,384,384]{2,1,0:T(8,128)S(1)} %get-tuple-element.5, f32[]{:T(128)} %div.22, f32[]{:T(128)} %bitcast.264), kind=kLoop, calls=%fused_computation.246 | loop fusion | flops 294912 | bytes 1769480 | tf_op jit(solution)/shard_map/vmap(vmap())/mul | solution.py:95
  28.2 1.4 convolution_bitcast_fusion.8
  29.6 0.4 fusion.44
  30.0 1.2 pad_maximum_fusion
  31.2 3.4 %collective-permute-start = (bf16[2,1,2,384,384]{4,3,0,2,1:T(8,128)(2,1)}, bf16[2,1,2,384,384]{4,3,0,2,1:T(8,128)(2,1)}, u32[]{:S(2)}, u32[]{:S(2)}) collective-permute-start(bf16[2,1,2,384,384]{4,3,0,2,1:T(8,128)(2,1)} %pad_maximum_fusion), channel_id=1, source_target_pairs={{0,4},{4,8},{8,12},{12,16},{16,20},{20,24},{24,28},{1,5},{5,9},{9,... | collective-permute-start | bytes 3538952 | tf_op jit(solution)/shard_map/ppermute | solution.py:17
  34.6 1.9 %fusion.141 = (bf16[1,2,1,2,384,384]{5,4,3,2,1,0:T(8,128)(2,1)S(1)}, bf16[1,2,1,2,384,384]{5,4,3,2,1,0:T(8,128)(2,1)S(1)}) fusion(bf16[2,2,1,2,384,384]{5,4,3,2,1,0:T(8,128)(2,1)} %param.8), kind=kLoop, calls=%fused_computation.281 | loop fusion | bytes 4718592 | tf_op jit(solution)/shard_map/slice | solution.py:158
  36.8 1.4 convolution_bitcast_fusion.7
  38.5 1.4 convolution_bitcast_fusion.6
  39.9 0.4 fusion.46
  40.3 1.4 convolution_bitcast_fusion.5
  42.0 1.4 convolution_bitcast_fusion.4
  43.4 0.4 fusion.48
  44.0 16.8 %collective-permute-start.1 = (bf16[2,1,2,384,384]{4,3,0,2,1:T(8,128)(2,1)S(1)}, bf16[2,1,2,384,384]{4,3,0,2,1:T(8,128)(2,1)S(1)}, u32[]{:S(2)}, u32[]{:S(2)}) collective-permute-start(bf16[2,1,2,384,384]{4,3,0,2,1:T(8,128)(2,1)S(1)} %pad_maximum_fusion.1), channel_id=1, source_target_pairs={{0,4},{4,8},{8,12},{12,16},{16,20},{20,24},{24,28},{1,5},{5,9},{9,... | collective-permute-start | bytes 3538952 | tf_op jit(solution)/shard_map/ppermute | solution.py:17
  61.2 1.8 collective-permute-done.1
  63.3 1.4 convolution_bitcast_fusion.3
  64.9 1.4 convolution_bitcast_fusion.2
  66.3 0.4 fusion.50
  66.7 1.4 convolution_bitcast_fusion.1
  68.4 1.4 convolution_bitcast_fusion
  69.8 0.4 fusion.53
  70.4 1.3 fusion.120
  71.8 0.7 all-reduce.2.cloned.1.call-update
  72.5 1.6 collective-permute-start.2
  74.1 40.6 %all-gather.2.cloned.1.call-done = bf16[4,1,384,384]{3,2,1,0:T(8,128)(2,1)} async-done(((bf16[1,1,384,384]{3,2,1,0:T(8,128)(2,1)}), bf16[4,1,384,384]{3,2,1,0:T(8,128)(2,1)}) %all-gather.2.cloned.1.call-update) | async-done | bytes 1179664 | tf_op jit(solution)/shard_map/all_gather | solution.py:163
  114.7 1.5 reduce_sum.51
  116.2 0.8 convert_reduce_fusion
  117.7 43.9 %all-reduce.2.cloned.1.call-done = bf16[1,384,384]{2,1,0:T(8,128)(2,1)} async-done(((bf16[1,384,384]{2,1,0:T(8,128)(2,1)}), bf16[1,384,384]{2,1,0:T(8,128)(2,1)}) %all-reduce.2.cloned.1.call-update) | async-done | bytes 294928 | tf_op jit(solution)/shard_map/psum | solution.py:166
  161.6 1.7 multiply_reduce_fusion
  164.0 1.1 bitcast_convert_fusion
  165.4 0.8 convolution_bitcast_fusion.15
  166.3 0.8 convolution_bitcast_fusion.12
  167.1 3.1 %subtract_convert_fusion.7 = (bf16[1,384,384]{1,2,0:T(8,128)(2,1)S(1)}, bf16[1,384,384]{1,2,0:T(8,128)(2,1)S(1)}) fusion(f32[384]{0:T(512)S(1)} %fusion.123, f32[]{:T(128)} %bitcast.11, f32[768,1,768]{0,2,1:T(8,128)S(1)} %convolution_bitcast_fusion.12), kind=kLoop, calls=%fused_computation.223 | loop fusion | flops 2801664 | bytes 2953220 | tf_op jit(solution)/shard_map/vmap()/convert_element_type | solution.py:73
  170.2 0.8 convolution_bitcast_fusion.14
  171.1 0.6 constant_dynamic-slice_fusion
  171.8 0.8 convolution_bitcast_fusion.13
  172.8 2.3 %fusion.118 = (bf16[1,1,384,384]{3,2,1,0:T(8,128)(2,1)S(1)}, bf16[1,1,384,384]{3,2,1,0:T(8,128)(2,1)S(1)}) fusion(f32[1,384,384]{2,1,0:T(8,128)S(1)} %copy-done.3, f32[]{:T(128)} %div.22, f32[]{:T(128)} %bitcast.265, f32[1,768,768]{2,1,0:T(8,128)S(1)} %convolution_bitcast_fusion.13), kind=kLoop, calls=%fused_computation.253 | loop fusion | flops 1769472 | bytes 3538952 | tf_op jit(solution)/shard_map/stack | solution.py:116
  175.2 0.9 maximum_bitcast_fusion.32
  (40 shorter events, 3.8 us)
Async XLA Ops:
  7.2 107.5 %all-gather.2.cloned.1.call-start = ((), (), s32[]{:S(2)}) async-start(), calls=%async_computation.1 | async-start | bytes 1474560 | tf_op jit(solution)/shard_map/all_gather | solution.py:163
  13.1 3.3 %copy-start.5 = (f32[1,384,384]{2,1,0:T(8,128)S(1)}, f32[1,384,384]{2,1,0:T(8,128)}, u32[]{:S(2)}) copy-start(f32[1,384,384]{2,1,0:T(8,128)} %param.13) | copy-start | bytes 1769476
  15.6 2.2 %copy-start.4 = (bf16[1,2,1,2,384,384]{5,4,3,2,1,0:T(8,128)(2,1)S(1)}, bf16[1,2,1,2,384,384]{5,4,3,2,1,0:T(8,128)(2,1)}, u32[]{:S(2)}) copy-start(bf16[1,2,1,2,384,384]{5,4,3,2,1,0:T(8,128)(2,1)} %param.7) | copy-start | bytes 3538948
  17.1 8.7 %copy-start.2 = (f32[1,384,384]{2,1,0:T(8,128)}, f32[1,384,384]{2,1,0:T(8,128)S(1)}, u32[]{:S(2)}) copy-start(f32[1,384,384]{2,1,0:T(8,128)S(1)} %get-tuple-element.5) | copy-start | bytes 1769476
  30.0 1.2 copy-start
  31.2 5.3 %collective-permute-start = (bf16[2,1,2,384,384]{4,3,0,2,1:T(8,128)(2,1)}, bf16[2,1,2,384,384]{4,3,0,2,1:T(8,128)(2,1)}, u32[]{:S(2)}, u32[]{:S(2)}) collective-permute-start(bf16[2,1,2,384,384]{4,3,0,2,1:T(8,128)(2,1)} %pad_maximum_fusion), channel_id=1, source_target_pairs={{0,4},{4,8},{8,12},{12,16},{16,20},{20,24},{24,28},{1,5},{5,9},{9,... | collective-permute-start | bytes 3538952 | tf_op jit(solution)/shard_map/ppermute | solution.py:17
  43.8 17.0 %copy-start.1 = (bf16[2,1,1,384,384]{4,3,0,2,1:T(8,128)(2,1)S(1)}, bf16[2,1,1,384,384]{4,3,0,2,1:T(8,128)(2,1)}, u32[]{:S(2)}) copy-start(bf16[2,1,1,384,384]{4,3,0,2,1:T(8,128)(2,1)} %copy-done) | copy-start | bytes 1769476
  44.0 19.0 %collective-permute-start.1 = (bf16[2,1,2,384,384]{4,3,0,2,1:T(8,128)(2,1)S(1)}, bf16[2,1,2,384,384]{4,3,0,2,1:T(8,128)(2,1)S(1)}, u32[]{:S(2)}, u32[]{:S(2)}) collective-permute-start(bf16[2,1,2,384,384]{4,3,0,2,1:T(8,128)(2,1)S(1)} %pad_maximum_fusion.1), channel_id=1, source_target_pairs={{0,4},{4,8},{8,12},{12,16},{16,20},{20,24},{24,28},{1,5},{5,9},{9,... | collective-permute-start | bytes 3538952 | tf_op jit(solution)/shard_map/ppermute | solution.py:17
  70.4 2.1 %copy-start.6 = (bf16[1,1,2,384,384]{4,3,2,1,0:T(8,128)(2,1)S(1)}, bf16[1,1,2,384,384]{4,3,2,1,0:T(8,128)(2,1)}, u32[]{:S(2)}) copy-start(bf16[1,1,2,384,384]{4,3,2,1,0:T(8,128)(2,1)} %param.9) | copy-start | bytes 1769476
  71.7 89.8 %all-reduce.2.cloned.1.call-start = ((), (), s32[]{:S(2)}) async-start(), calls=%async_computation | async-start | bytes 589824 | tf_op jit(solution)/shard_map/psum | solution.py:166
  72.5 92.6 %collective-permute-start.2 = (bf16[1,2,384,384]{3,2,1,0:T(8,128)(2,1)S(1)}, bf16[1,2,384,384]{3,2,1,0:T(8,128)(2,1)S(1)}, u32[]{:S(2)}, u32[]{:S(2)}) collective-permute-start(bf16[1,2,384,384]{3,2,1,0:T(8,128)(2,1)S(1)} %bitcast.268), channel_id=1, source_target_pairs={{4,0},{8,4},{12,8},{16,12},{20,16},{24,20},{28,24},{5,1},{9,5},{13... | collective-permute-start | bytes 1769480 | tf_op jit(solution)/shard_map/ppermute | solution.py:17
  171.8 1.1 copy-start.3
Sparse Core Ops, SparseCore 0:
  71.9 42.7 all-gather.1
  118.2 43.3 all-reduce.1
